TPU v7x, 256 devices: a whole 4x4x8 slice. The times are simulated.
256 devices in a mesh: row: 8 (over y, core), col: 32 (over z, x).
Axes of the slice: x: 4, y: 4, z: 8, core: 2. Of those that a mesh axis runs over, the one named last changes fastest.
Arguments:
- solution: float32 [8, 32, 16, 128, 128], P('row', 'col'), may hold values from -6 to 6
- residual: float32 [8, 32, 16, 128, 128], P('row', 'col'), may hold values from -6 to 6, as said below
- prev_direction: float32 [8, 32, 16, 128, 128], P('row', 'col'), may hold values from -6 to 6, as said below
- prev_dot: float32 [128], replicated, may hold values from 262144 to 1048576
- face_lists: int32 [8, 32, 4, 4], P('row', 'col'), may hold values from 0 to 16, as said below
- multiplicity: int32 [8, 32, 16], P('row', 'col'), may hold values from 1 to 2, as said below
- block_pattern: int32 [8, 32, 16, 3], P('row', 'col'), may hold values from 0 to 15, as said below
- schur: float32 [8, 32, 16, 3, 128, 128], P('row', 'col'), may hold values from -1 to 4, as said below
- neumann_inverse: float32 [8, 32, 16, 3, 128, 128], P('row', 'col'), may hold values from 0 to 2, as said below
- coarse_basis: float32 [8, 32, 8, 2048], P('row', 'col'), may hold values from -0.25 to 0.25
- primal_map: int32 [8, 32, 8], P('row', 'col'), may hold values from 0 to 1023, all different within a row
- coarse_inverse: float32 [1024, 1024], P('col'), may hold values from -1 to 1, as said below
Outputs:
- new_solution: float32 [8, 32, 16, 128, 128], P('row', 'col')
- new_residual: float32 [8, 32, 16, 128, 128], P('row', 'col')
- direction: float32 [8, 32, 16, 128, 128], P('row', 'col')
Inputs may be any that keep to these rules, and one draw needn't show every extreme that they name: face_lists[i, j, f, k] names the interface blocks that subdomain (i, j) shares with its neighbour across face f (0 toward row i-1, 1 toward row i+1, 2 toward column j-1, 3 toward column j+1); slot k of a face names the same unknowns as slot k of the neighbour's list for the facing face, and both lists have the same length, 1 to 4 blocks, none on faces at the grid's edge; unused slots hold 16; no block lies on two faces; some face holds 4 blocks. multiplicity is 2 for blocks named in face_lists and 1 for the others. block_pattern[i, j, b, 0] = b; the two other entries of block row b are two other blocks, each of which lists b in turn. `schur`: each subdomain's Schur complement is symmetric positive definite, with positive diagonal and no positive entry off it. `neumann_inverse`: each subdomain's local solve matrix is symmetric positive definite. `coarse_inverse`: symmetric positive definite. `residual`: copies of an unknown held by two subdomains (slot k of facing lists) are equal. `prev_direction`: copies of an unknown held by two subdomains (slot k of facing lists) are equal.
All inputs are finite; a program needn't handle non-finite values.
Results may differ from a plain program's by a relative error of at most 0.0003.
Values sent between devices are 32-bit elements; how exact they have to be, the bound alone decides.
A program may use at most 128 MiB of HBM per device.

v0:
```python
import jax
import jax.numpy as jnp
from jax import lax
from jax.sharding import PartitionSpec as P

HIGH = lax.Precision.HIGHEST


def extended(cells, sides, width):
    for axis, dim in sides:
        count = lax.axis_size(axis)
        ends = count - 1
        head = lax.slice_in_dim(cells, 0, width, axis=dim)
        tail = lax.slice_in_dim(cells, cells.shape[dim] - width, cells.shape[dim], axis=dim)
        cells = jnp.concatenate(
            [
                lax.ppermute(tail, axis, [(i, (i + 1) % count) for i in range(ends)]),
                cells,
                lax.ppermute(head, axis, [((i + 1) % count, i) for i in range(ends)]),
            ],
            axis=dim,
        )
    return cells


def block_product(blocks, pattern, values_in):
    stacked_count, block_count, dofs, cases = values_in.shape
    gathered = jnp.take(values_in, pattern.reshape(-1), axis=1)
    gathered = gathered.reshape(stacked_count, block_count, pattern.shape[1], dofs, cases)
    return jnp.einsum("bkij,vbkjn->vbin", blocks, gathered, precision=HIGH)


def assemble(values_in, faces):
    stacked_count, block_count, dofs, cases = values_in.shape
    flattened = values_in.reshape(stacked_count, block_count, dofs * cases)
    indicator = (faces[..., None] == jnp.arange(block_count)).astype(jnp.float32)
    face_values = jnp.einsum("fkb,vbc->fvkc", indicator, flattened, precision=HIGH)
    row_faces = extended(face_values[0:2], (("row", 0),), 1)
    col_faces = extended(face_values[2:4], (("col", 0),), 1)
    received = jnp.stack([row_faces[0], row_faces[3], col_faces[0], col_faces[3]])
    added = jnp.einsum("fkb,fvkc->vbc", indicator, received, precision=HIGH)
    return (flattened + added).reshape(values_in.shape)


def precondition(residual, weight, faces, pattern, neumann, basis, primal_map, inverse_rows):
    scaled = residual * weight
    local_term = block_product(neumann, pattern, scaled[None])[0]
    cases = residual.shape[-1]
    coarse_local = jnp.dot(basis, scaled.reshape(-1, cases), precision=HIGH)
    owned_count, coarse_total_rows = inverse_rows.shape
    indicator = (primal_map[:, None] == jnp.arange(coarse_total_rows)).astype(jnp.float32)
    owned_rhs = lax.psum_scatter(
        jnp.dot(indicator.T, coarse_local, precision=HIGH), "col", scatter_dimension=0, tiled=True
    )
    owned_rhs = lax.psum(owned_rhs, "row")
    columns = inverse_rows
    owned_solution = jnp.dot(
        columns, lax.all_gather(owned_rhs, "col", axis=0, tiled=True), precision=HIGH
    )
    columns = indicator
    own_coarse = jnp.dot(
        columns, lax.all_gather(owned_solution, "col", axis=0, tiled=True), precision=HIGH
    )
    coarse_back = jnp.dot(basis.T, own_coarse, precision=HIGH).reshape(residual.shape)
    return assemble(((local_term + coarse_back) * weight)[None], faces)[0]


def per_device(
    solution,
    residual,
    prev_direction,
    prev_dot,
    face_lists,
    multiplicity,
    block_pattern,
    schur,
    neumann_inverse,
    coarse_basis,
    primal_map,
    coarse_inverse,
):
    faces = face_lists[0, 0]
    pattern = block_pattern[0, 0]
    weight = (1.0 / multiplicity[0, 0].astype(jnp.float32))[:, None, None]
    current = residual[0, 0]
    previous = prev_direction[0, 0]
    precond = precondition(
        current,
        weight,
        faces,
        pattern,
        neumann_inverse[0, 0],
        coarse_basis[0, 0],
        primal_map[0, 0],
        coarse_inverse,
    )
    local_precond_dot = jnp.sum(current * precond * weight, axis=(0, 1))
    precond_dot = lax.psum(local_precond_dot, ("row", "col"))
    direction_mix = precond_dot / prev_dot
    direction = precond + direction_mix * previous
    image = assemble(block_product(schur[0, 0], pattern, direction[None]), faces)[0]
    curvature = lax.psum(jnp.sum(direction * image * weight, axis=(0, 1)), ("row", "col"))
    step_size = precond_dot / curvature
    new_solution = solution[0, 0] + step_size * direction
    new_residual = current - step_size * image
    return (new_solution[None, None], new_residual[None, None], direction[None, None])


def solution(mesh):
    placed = (
        P("row", "col", None, None, None),
        P("row", "col", None, None, None),
        P("row", "col", None, None, None),
        P(),
        P("row", "col", None, None),
        P("row", "col", None),
        P("row", "col", None, None),
        P("row", "col", None, None, None, None),
        P("row", "col", None, None, None, None),
        P("row", "col", None, None),
        P("row", "col", None),
        P("col", None),
    )
    return jax.shard_map(
        per_device,
        mesh=mesh,
        in_specs=placed,
        out_specs=(
            P("row", "col", None, None, None),
            P("row", "col", None, None, None),
            P("row", "col", None, None, None),
        ),
        check_vma=False,
    )
```

profile of v0, /device:TPU:1, one launch (start us, length us, event | category | flops | bytes accessed | tf_op | source)
XLA Modules:
  0.0 597.9 jit_solution(11276702184320067996)
XLA Ops:
  12.5 2.3 fusion.31
  15.1 3.6 gather_fusion
  20.9 6.2 %fusion.6 = f32[1,16,128,128]{2,3,1,0:T(8,128)} fusion(f32[16,3,128,128]{3,2,1,0:T(8,128)S(1)} %bitcast.147, f32[1,1,16,3,128,128]{5,4,3,2,1,0:T(8,128)S(1)} %copy-done), kind=kOutput, calls=%fused_computation.15 | convolution fusion | flops 1207959552 | bytes 7340032 | tf_op jit(solution)/shard_map/bkij,vbkjn->vbin/dot_general | solution.py:30
  27.1 2.6 copy.44
  29.7 194.6 %reduce-scatter.2.cloned.1.call-done = f32[32,128]{1,0:T(8,128)} async-done(((f32[1024,128]{1,0:T(8,128)}), f32[32,128]{1,0:T(8,128)}) %reduce-scatter.2.cloned.1.call-update) | async-done | bytes 16400 | tf_op jit(solution)/shard_map/reduce_scatter | solution.py:52
  224.3 26.4 %psum.21 = f32[32,128]{1,0:T(8,128)S(1)} all-reduce(f32[32,128]{1,0:T(8,128)} %reduce-scatter.2.cloned.1.call-done), channel_id=1, replica_groups=mesh['row'=8,'col'=32] {'row'}, use_global_device_ids=true, to_apply=%region_1.3 | all-reduce | flops 4096 | bytes 32768 | tf_op jit(solution)/shard_map/psum | solution.py:55
  250.7 35.9 %all_gather.6 = f32[1024,128]{1,0:T(8,128)S(1)} all-gather(f32[32,128]{1,0:T(8,128)S(1)} %psum.21), channel_id=1, replica_groups=mesh['row'=8,'col'=32] {'col'}, dimensions={0}, use_global_device_ids=true | all-gather | bytes 540672 | tf_op jit(solution)/shard_map/all_gather | solution.py:58
  287.0 35.8 %all_gather.7 = f32[1024,128]{1,0:T(8,128)S(1)} all-gather(f32[32,128]{1,0:T(8,128)S(1)} %convolution_bitcast_fusion.5), channel_id=1, replica_groups=mesh['row'=8,'col'=32] {'col'}, dimensions={0}, use_global_device_ids=true | all-gather | bytes 540672 | tf_op jit(solution)/shard_map/all_gather | solution.py:62
  325.0 2.5 copy.42
  327.6 2.4 reshape.184
  329.9 3.0 convolution_bitcast_fusion.3
  333.9 27.6 %collective-permute-start = (f32[1,1,4,16384]{3,2,0,1:T(4,128)}, f32[1,1,4,16384]{3,2,0,1:T(4,128)}, u32[]{:S(2)}, u32[]{:S(2)}) collective-permute-start(f32[1,1,4,16384]{3,2,0,1:T(4,128)} %get-tuple-element.10), channel_id=1, source_target_pairs={{0,32},{32,64},{64,96},{96,128},{128,160},{160,192},{192,224},{1,3... | collective-permute-start | bytes 786440 | tf_op jit(solution)/shard_map/ppermute | solution.py:17
  361.5 3.8 collective-permute-start.1
  365.4 3.1 collective-permute-start.2
  369.7 2.5 copy.41
  372.2 2.4 squeeze.32
  374.6 2.4 reshape.183
  378.6 3.4 fusion.1
  384.5 78.4 %psum.22 = f32[128]{0:T(128)S(1)} all-reduce(f32[128]{0:T(128)S(1)} %fusion.14), channel_id=1, replica_groups=mesh['row'=8,'col'=32] {'row','col'}, use_global_device_ids=true, to_apply=%region_3.5 | all-reduce | flops 128 | bytes 1024 | tf_op jit(solution)/shard_map/psum | solution.py:98
  462.9 2.7 fusion.12
  465.5 3.6 gather_fusion.1
  469.1 2.3 bitcast_select_fusion
  472.0 6.3 %fusion.9 = f32[1,16,128,128]{2,3,1,0:T(8,128)} fusion(f32[16,3,128,128]{3,2,1,0:T(8,128)S(1)} %bitcast.146, f32[1,1,16,3,128,128]{5,4,3,2,1,0:T(8,128)S(1)} %copy-done.7), kind=kOutput, calls=%fused_computation.16 | convolution fusion | flops 1207959552 | bytes 7340032 | tf_op jit(solution)/shard_map/bkij,vbkjn->vbin/dot_general | solution.py:30
  478.3 2.5 copy.47
  480.8 2.4 reshape.224
  483.2 2.4 reshape.187
  485.6 2.4 convolution_bitcast_fusion.1
  488.1 3.7 collective-permute-start.4
  497.0 2.5 collective-permute-done.5
  501.7 4.1 collective-permute-done.7
  508.2 78.4 %psum.23 = f32[128]{0:T(128)S(1)} all-reduce(f32[128]{0:T(128)S(1)} %bitcast_reduce_fusion), channel_id=1, replica_groups=mesh['row'=8,'col'=32] {'row','col'}, use_global_device_ids=true, to_apply=%region_6.8 | all-reduce | flops 128 | bytes 1024 | tf_op jit(solution)/shard_map/psum | solution.py:102
  586.6 4.5 multiply_add_fusion
  (63 shorter events, 27.0 us)
Async XLA Ops:
  7.2 13.7 %copy-start = (f32[1,1,16,3,128,128]{5,4,3,2,1,0:T(8,128)S(1)}, f32[1,1,16,3,128,128]{5,4,3,2,1,0:T(8,128)}, u32[]{:S(2)}) copy-start(f32[1,1,16,3,128,128]{5,4,3,2,1,0:T(8,128)} %param.22) | copy-start | bytes 9437188
  7.2 3.8 copy-start.11
  7.2 217.1 %reduce-scatter.2.cloned.1.call-start = ((), (), s32[]{:S(2)}) async-start(), calls=%async_computation.1 | async-start | bytes 540672 | tf_op jit(solution)/shard_map/reduce_scatter | solution.py:52
  8.0 6.8 %copy-start.12 = (s32[1,1,16,3]{2,1,3,0:T(1,128)S(1)}, s32[1,1,16,3]{2,1,3,0:T(1,128)}, u32[]{:S(2)}) copy-start(s32[1,1,16,3]{2,1,3,0:T(1,128)} %param.20) | copy-start | bytes 580
  20.9 265.7 %copy-start.9 = (f32[32,1024]{1,0:T(8,128)S(1)}, f32[32,1024]{1,0:T(8,128)}, u32[]{:S(2)}) copy-start(f32[32,1024]{1,0:T(8,128)} %param.25) | copy-start | bytes 393220
  27.1 295.9 %copy-start.8 = (f32[1,1,8,2048]{3,2,1,0:T(8,128)S(1)}, f32[1,1,8,2048]{3,2,1,0:T(8,128)}, u32[]{:S(2)}) copy-start(f32[1,1,8,2048]{3,2,1,0:T(8,128)} %param.23) | copy-start | bytes 196612
  286.9 43.0 %copy-start.10 = (s32[1,1,4,4]{3,2,1,0:T(4,128)S(1)}, s32[1,1,4,4]{3,2,1,0:T(4,128)}, u32[]{:S(2)}) copy-start(s32[1,1,4,4]{3,2,1,0:T(4,128)} %param.18) | copy-start | bytes 196
  333.9 43.1 %collective-permute-start = (f32[1,1,4,16384]{3,2,0,1:T(4,128)}, f32[1,1,4,16384]{3,2,0,1:T(4,128)}, u32[]{:S(2)}, u32[]{:S(2)}) collective-permute-start(f32[1,1,4,16384]{3,2,0,1:T(4,128)} %get-tuple-element.10), channel_id=1, source_target_pairs={{0,32},{32,64},{64,96},{96,128},{128,160},{160,192},{192,224},{1,3... | collective-permute-start | bytes 786440 | tf_op jit(solution)/shard_map/ppermute | solution.py:17
  361.5 15.5 %collective-permute-start.1 = (f32[1,1,4,16384]{3,2,0,1:T(4,128)}, f32[1,1,4,16384]{3,2,0,1:T(4,128)}, u32[]{:S(2)}, u32[]{:S(2)}) collective-permute-start(f32[1,1,4,16384]{3,2,0,1:T(4,128)} %get-tuple-element.13), channel_id=1, source_target_pairs={{32,0},{64,32},{96,64},{128,96},{160,128},{192,160},{224,192},{33,... | collective-permute-start | bytes 786440 | tf_op jit(solution)/shard_map/ppermute | solution.py:19
  365.4 11.7 %collective-permute-start.2 = (f32[1,1,4,16384]{3,2,0,1:T(4,128)}, f32[1,1,4,16384]{3,2,0,1:T(4,128)}, u32[]{:S(2)}, u32[]{:S(2)}) collective-permute-start(f32[1,1,4,16384]{3,2,0,1:T(4,128)} %get-tuple-element.12), channel_id=1, source_target_pairs={{0,1},{1,2},{2,3},{3,4},{4,5},{5,6},{6,7},{7,8},{8,9},{9,10},{10,1... | collective-permute-start | bytes 786440 | tf_op jit(solution)/shard_map/ppermute | solution.py:17
  368.4 10.2 %collective-permute-start.3 = (f32[1,1,4,16384]{3,2,0,1:T(4,128)S(1)}, f32[1,1,4,16384]{3,2,0,1:T(4,128)}, u32[]{:S(2)}, u32[]{:S(2)}) collective-permute-start(f32[1,1,4,16384]{3,2,0,1:T(4,128)S(1)} %get-tuple-element.11), channel_id=1, source_target_pairs={{1,0},{2,1},{3,2},{4,3},{5,4},{6,5},{7,6},{8,7},{9,8},{10,9},{11,1... | collective-permute-start | bytes 786440 | tf_op jit(solution)/shard_map/ppermute | solution.py:19
  378.6 5.5 copy-start.1
  382.0 1.0 copy-start.4
  382.0 80.9 %copy-start.13 = (f32[128]{0:T(128)S(1)}, f32[128]{0:T(128)}, u32[]{:S(2)}) copy-start(f32[128]{0:T(128)} %param.17) | copy-start | bytes 1540
  383.2 1.0 copy-start.2
  469.1 2.8 copy-start.7
  485.6 20.1 %copy-start.3 = (f32[1,16,16384]{2,1,0:T(8,128)S(1)}, f32[1,16,16384]{2,1,0:T(8,128)}, u32[]{:S(2)}) copy-start(f32[1,16,16384]{2,1,0:T(8,128)} %squeeze.32) | copy-start | bytes 3145732
  485.6 20.1 %copy-start.5 = (f32[1,16,16384]{2,1,0:T(8,128)S(1)}, f32[1,16,16384]{2,1,0:T(8,128)}, u32[]{:S(2)}) copy-start(f32[1,16,16384]{2,1,0:T(8,128)} %copy-done.4) | copy-start | bytes 3145732
  485.6 20.1 %copy-start.6 = (f32[1,16,16384]{2,1,0:T(8,128)S(1)}, f32[1,16,16384]{2,1,0:T(8,128)}, u32[]{:S(2)}) copy-start(f32[1,16,16384]{2,1,0:T(8,128)} %reshape.187) | copy-start | bytes 3145732
  488.1 8.9 %collective-permute-start.4 = (f32[1,1,4,16384]{3,2,0,1:T(4,128)S(1)}, f32[1,1,4,16384]{3,2,0,1:T(4,128)S(1)}, u32[]{:S(2)}, u32[]{:S(2)}) collective-permute-start(f32[1,1,4,16384]{3,2,0,1:T(4,128)S(1)} %get-tuple-element.6), channel_id=1, source_target_pairs={{0,32},{32,64},{64,96},{96,128},{128,160},{160,192},{192,224},{1,3... | collective-permute-start | bytes 786440 | tf_op jit(solution)/shard_map/ppermute | solution.py:17
  491.8 7.7 %collective-permute-start.5 = (f32[1,1,4,16384]{3,2,0,1:T(4,128)S(1)}, f32[1,1,4,16384]{3,2,0,1:T(4,128)S(1)}, u32[]{:S(2)}, u32[]{:S(2)}) collective-permute-start(f32[1,1,4,16384]{3,2,0,1:T(4,128)S(1)} %get-tuple-element.9), channel_id=1, source_target_pairs={{32,0},{64,32},{96,64},{128,96},{160,128},{192,160},{224,192},{33,... | collective-permute-start | bytes 786440 | tf_op jit(solution)/shard_map/ppermute | solution.py:19
  493.7 7.9 %collective-permute-start.6 = (f32[1,1,4,16384]{3,2,0,1:T(4,128)S(1)}, f32[1,1,4,16384]{3,2,0,1:T(4,128)S(1)}, u32[]{:S(2)}, u32[]{:S(2)}) collective-permute-start(f32[1,1,4,16384]{3,2,0,1:T(4,128)S(1)} %get-tuple-element.8), channel_id=1, source_target_pairs={{0,1},{1,2},{2,3},{3,4},{4,5},{5,6},{6,7},{7,8},{8,9},{9,10},{10,1... | collective-permute-start | bytes 786440 | tf_op jit(solution)/shard_map/ppermute | solution.py:17
  495.7 10.1 %collective-permute-start.7 = (f32[1,1,4,16384]{3,2,0,1:T(4,128)S(1)}, f32[1,1,4,16384]{3,2,0,1:T(4,128)S(1)}, u32[]{:S(2)}, u32[]{:S(2)}) collective-permute-start(f32[1,1,4,16384]{3,2,0,1:T(4,128)S(1)} %get-tuple-element.7), channel_id=1, source_target_pairs={{1,0},{2,1},{3,2},{4,3},{5,4},{6,5},{7,6},{8,7},{9,8},{10,9},{11,1... | collective-permute-start | bytes 786440 | tf_op jit(solution)/shard_map/ppermute | solution.py:19
Sparse Core Ops, SparseCore 0:
  12.7 211.5 reduce-scatter.1
where the time goes:
time: 599 us; the launch traced here: 598 us
  blocking collectives  255 us (43%)
  waiting for transfers between devices  205 us (34%)
  starting transfers between devices  44.6 us (7%)
  local copies, waits for them, and re-layouts  34.4 us (6%)
  matrix products  28.1 us (5%)
  other arithmetic  16.6 us (3%)
  between operations  14.3 us (2%)
    reduce_scatter x1, waiting for transfers between devices, precondition(): lax.psum_scatter(jnp.dot(indicator.T, coarse_local, precision=HIGH), 'col...  195 us
    psum x1, blocking collectives, per_device(): lax.psum(jnp.sum(direction * image * weight, axis=(0, 1)), ('row', 'col'))  78.4 us
    psum x1, blocking collectives, per_device(): precond_dot = lax.psum(local_precond_dot, ('row', 'col'))  78.4 us
    ppermute x4, starting transfers between devices, extended(): lax.ppermute(tail, axis, [(i, (i + 1) % count) for i in range(ends)])  36.3 us
    all_gather x1, blocking collectives, precondition(): lax.all_gather(owned_rhs, 'col', axis=0, tiled=True)  35.9 us
    all_gather x1, blocking collectives, precondition(): lax.all_gather(owned_solution, 'col', axis=0, tiled=True)  35.8 us
    psum x1, blocking collectives, precondition(): owned_rhs = lax.psum(owned_rhs, 'row')  26.4 us
    dot_general x2, matrix products, block_product(): return jnp.einsum('bkij,vbkjn->vbin', blocks, gathered, precision=HIGH)  12.5 us
  transfers between devices with their start and end apart: 9, of which 5 were waited for; matrix products, arithmetic and copies ran while one was open for 4% of the time, Pallas kernels for 0%

commit v1 on v0

--- a/solution.py
+++ b/solution.py
@@ -4,6 +4,7 @@
 from jax.sharding import PartitionSpec as P
 
 HIGH = lax.Precision.HIGHEST
+fill_pages_over_axis = lambda v0: lax.all_gather(v0, axis_name=("row", "col")).sum(axis=0)
 
 
 def extended(cells, sides, width):
@@ -95,7 +96,7 @@
         coarse_inverse,
     )
     local_precond_dot = jnp.sum(current * precond * weight, axis=(0, 1))
-    precond_dot = lax.psum(local_precond_dot, ("row", "col"))
+    precond_dot = fill_pages_over_axis(local_precond_dot)
     direction_mix = precond_dot / prev_dot
     direction = precond + direction_mix * previous
     image = assemble(block_product(schur[0, 0], pattern, direction[None]), faces)[0]

time: 599 us -> 577 us (0.963)
  blocking collectives: 255 us -> 232 us
    psum x1 -> x0, blocking collectives: 78.4 us -> none  [per_device(): precond_dot = lax.psum(local_precond_dot, ('row', 'col'))]
    all_gather x0 -> x1, blocking collectives: none -> 56.4 us  [lax.all_gather(v0, axis_name=('row', 'col')).sum(axis=0)]
where the time goes in v1:
time: 577 us; the launch traced here: 576 us
  blocking collectives  232 us (40%)
  waiting for transfers between devices  206 us (36%)
  starting transfers between devices  45.7 us (8%)
  local copies, waits for them, and re-layouts  33.2 us (6%)
  matrix products  28.1 us (5%)
  other arithmetic  16.9 us (3%)
  between operations  14.3 us (2%)
    reduce_scatter x1, waiting for transfers between devices, precondition(): lax.psum_scatter(jnp.dot(indicator.T, coarse_local, precision=HIGH), 'col...  195 us
    psum x1, blocking collectives, per_device(): lax.psum(jnp.sum(direction * image * weight, axis=(0, 1)), ('row', 'col'))  77.5 us
    all_gather x1, blocking collectives, lax.all_gather(v0, axis_name=('row', 'col')).sum(axis=0)  56.4 us
    ppermute x4, starting transfers between devices, extended(): lax.ppermute(tail, axis, [(i, (i + 1) % count) for i in range(ends)])  37.2 us
    all_gather x1, blocking collectives, precondition(): lax.all_gather(owned_rhs, 'col', axis=0, tiled=True)  35.9 us
    all_gather x1, blocking collectives, precondition(): lax.all_gather(owned_solution, 'col', axis=0, tiled=True)  35.8 us
    psum x1, blocking collectives, precondition(): owned_rhs = lax.psum(owned_rhs, 'row')  26.4 us
    dot_general x2, matrix products, block_product(): return jnp.einsum('bkij,vbkjn->vbin', blocks, gathered, precision=HIGH)  12.5 us
  transfers between devices with their start and end apart: 9, of which 5 were waited for; matrix products, arithmetic and copies ran while one was open for 4% of the time, Pallas kernels for 0%

profile of v1, /device:TPU:1, one launch (start us, length us, event | category | flops | bytes accessed | tf_op | source)
XLA Modules:
  0.0 576.0 jit_solution(15737009238192076865)
XLA Ops:
  12.5 2.3 fusion.31
  15.1 3.6 gather_fusion
  20.9 6.2 %fusion.6 = f32[1,16,128,128]{2,3,1,0:T(8,128)} fusion(f32[16,3,128,128]{3,2,1,0:T(8,128)S(1)} %bitcast.148, f32[1,1,16,3,128,128]{5,4,3,2,1,0:T(8,128)S(1)} %copy-done), kind=kOutput, calls=%fused_computation.15 | convolution fusion | flops 1207959552 | bytes 7340032 | tf_op jit(solution)/shard_map/bkij,vbkjn->vbin/dot_general | solution.py:31
  27.1 2.6 copy.44
  29.7 194.6 %reduce-scatter.2.cloned.1.call-done = f32[32,128]{1,0:T(8,128)} async-done(((f32[1024,128]{1,0:T(8,128)}), f32[32,128]{1,0:T(8,128)}) %reduce-scatter.2.cloned.1.call-update) | async-done | bytes 16400 | tf_op jit(solution)/shard_map/reduce_scatter | solution.py:53
  224.3 26.4 %psum.14 = f32[32,128]{1,0:T(8,128)S(1)} all-reduce(f32[32,128]{1,0:T(8,128)} %reduce-scatter.2.cloned.1.call-done), channel_id=1, replica_groups=mesh['row'=8,'col'=32] {'row'}, use_global_device_ids=true, to_apply=%region_1.3 | all-reduce | flops 4096 | bytes 32768 | tf_op jit(solution)/shard_map/psum | solution.py:56
  250.7 35.9 %all_gather.12 = f32[1024,128]{1,0:T(8,128)S(1)} all-gather(f32[32,128]{1,0:T(8,128)S(1)} %psum.14), channel_id=1, replica_groups=mesh['row'=8,'col'=32] {'col'}, dimensions={0}, use_global_device_ids=true | all-gather | bytes 540672 | tf_op jit(solution)/shard_map/all_gather | solution.py:59
  287.0 35.8 %all_gather.13 = f32[1024,128]{1,0:T(8,128)S(1)} all-gather(f32[32,128]{1,0:T(8,128)S(1)} %convolution_bitcast_fusion.5), channel_id=1, replica_groups=mesh['row'=8,'col'=32] {'col'}, dimensions={0}, use_global_device_ids=true | all-gather | bytes 540672 | tf_op jit(solution)/shard_map/all_gather | solution.py:63
  325.0 2.5 copy.42
  327.6 2.4 reshape.184
  329.9 3.0 convolution_bitcast_fusion.3
  333.9 27.6 %collective-permute-start = (f32[1,1,4,16384]{3,2,0,1:T(4,128)}, f32[1,1,4,16384]{3,2,0,1:T(4,128)}, u32[]{:S(2)}, u32[]{:S(2)}) collective-permute-start(f32[1,1,4,16384]{3,2,0,1:T(4,128)} %get-tuple-element.10), channel_id=1, source_target_pairs={{0,32},{32,64},{64,96},{96,128},{128,160},{160,192},{192,224},{1,3... | collective-permute-start | bytes 786440 | tf_op jit(solution)/shard_map/ppermute | solution.py:18
  361.5 3.8 collective-permute-start.1
  365.4 3.1 collective-permute-start.2
  369.7 2.5 copy.41
  372.2 2.4 squeeze.32
  374.6 2.4 reshape.183
  378.6 3.4 fusion.1
  383.3 56.4 %all-gather.1 = f32[256,1,128]{2,1,0:T(1,128)S(1)} all-gather(f32[1,1,128]{2,1,0:T(1,128)S(1)} %bitcast.161), channel_id=2, replica_groups=mesh['row'=8,'col'=32] {'row','col'}, dimensions={0}, use_global_device_ids=true | all-gather | bytes 131584 | tf_op jit(solution)/shard_map/all_gather | solution.py:7
  440.0 2.7 fusion.12
  442.6 3.6 gather_fusion.1
  446.2 2.3 bitcast_select_fusion
  449.1 6.3 %fusion.9 = f32[1,16,128,128]{2,3,1,0:T(8,128)} fusion(f32[16,3,128,128]{3,2,1,0:T(8,128)S(1)} %bitcast.147, f32[1,1,16,3,128,128]{5,4,3,2,1,0:T(8,128)S(1)} %copy-done.7), kind=kOutput, calls=%fused_computation.16 | convolution fusion | flops 1207959552 | bytes 7340032 | tf_op jit(solution)/shard_map/bkij,vbkjn->vbin/dot_general | solution.py:31
  455.4 2.5 copy.47
  457.9 2.4 reshape.228
  460.3 2.4 reshape.187
  462.7 2.4 convolution_bitcast_fusion.1
  465.2 5.2 collective-permute-start.4
  475.2 3.0 collective-permute-done.5
  479.5 5.2 collective-permute-done.7
  487.1 77.5 %psum.15 = f32[128]{0:T(128)S(1)} all-reduce(f32[128]{0:T(128)S(1)} %bitcast_reduce_fusion), channel_id=1, replica_groups=mesh['row'=8,'col'=32] {'row','col'}, use_global_device_ids=true, to_apply=%region_6.8 | all-reduce | flops 128 | bytes 1024 | tf_op jit(solution)/shard_map/psum | solution.py:103
  564.7 4.5 multiply_add_fusion
  (64 shorter events, 24.8 us)
Async XLA Ops:
  7.2 13.7 %copy-start = (f32[1,1,16,3,128,128]{5,4,3,2,1,0:T(8,128)S(1)}, f32[1,1,16,3,128,128]{5,4,3,2,1,0:T(8,128)}, u32[]{:S(2)}) copy-start(f32[1,1,16,3,128,128]{5,4,3,2,1,0:T(8,128)} %param.22) | copy-start | bytes 9437188
  7.2 3.8 copy-start.11
  7.2 217.1 %reduce-scatter.2.cloned.1.call-start = ((), (), s32[]{:S(2)}) async-start(), calls=%async_computation.1 | async-start | bytes 540672 | tf_op jit(solution)/shard_map/reduce_scatter | solution.py:53
  8.0 6.8 %copy-start.12 = (s32[1,1,16,3]{2,1,3,0:T(1,128)S(1)}, s32[1,1,16,3]{2,1,3,0:T(1,128)}, u32[]{:S(2)}) copy-start(s32[1,1,16,3]{2,1,3,0:T(1,128)} %param.20) | copy-start | bytes 580
  20.9 265.7 %copy-start.9 = (f32[32,1024]{1,0:T(8,128)S(1)}, f32[32,1024]{1,0:T(8,128)}, u32[]{:S(2)}) copy-start(f32[32,1024]{1,0:T(8,128)} %param.25) | copy-start | bytes 393220
  27.1 295.9 %copy-start.8 = (f32[1,1,8,2048]{3,2,1,0:T(8,128)S(1)}, f32[1,1,8,2048]{3,2,1,0:T(8,128)}, u32[]{:S(2)}) copy-start(f32[1,1,8,2048]{3,2,1,0:T(8,128)} %param.23) | copy-start | bytes 196612
  286.9 43.0 %copy-start.10 = (s32[1,1,4,4]{3,2,1,0:T(4,128)S(1)}, s32[1,1,4,4]{3,2,1,0:T(4,128)}, u32[]{:S(2)}) copy-start(s32[1,1,4,4]{3,2,1,0:T(4,128)} %param.18) | copy-start | bytes 196
  333.9 43.1 %collective-permute-start = (f32[1,1,4,16384]{3,2,0,1:T(4,128)}, f32[1,1,4,16384]{3,2,0,1:T(4,128)}, u32[]{:S(2)}, u32[]{:S(2)}) collective-permute-start(f32[1,1,4,16384]{3,2,0,1:T(4,128)} %get-tuple-element.10), channel_id=1, source_target_pairs={{0,32},{32,64},{64,96},{96,128},{128,160},{160,192},{192,224},{1,3... | collective-permute-start | bytes 786440 | tf_op jit(solution)/shard_map/ppermute | solution.py:18
  361.5 15.5 %collective-permute-start.1 = (f32[1,1,4,16384]{3,2,0,1:T(4,128)}, f32[1,1,4,16384]{3,2,0,1:T(4,128)}, u32[]{:S(2)}, u32[]{:S(2)}) collective-permute-start(f32[1,1,4,16384]{3,2,0,1:T(4,128)} %get-tuple-element.13), channel_id=1, source_target_pairs={{32,0},{64,32},{96,64},{128,96},{160,128},{192,160},{224,192},{33,... | collective-permute-start | bytes 786440 | tf_op jit(solution)/shard_map/ppermute | solution.py:20
  365.4 11.7 %collective-permute-start.2 = (f32[1,1,4,16384]{3,2,0,1:T(4,128)}, f32[1,1,4,16384]{3,2,0,1:T(4,128)}, u32[]{:S(2)}, u32[]{:S(2)}) collective-permute-start(f32[1,1,4,16384]{3,2,0,1:T(4,128)} %get-tuple-element.12), channel_id=1, source_target_pairs={{0,1},{1,2},{2,3},{3,4},{4,5},{5,6},{6,7},{7,8},{8,9},{9,10},{10,1... | collective-permute-start | bytes 786440 | tf_op jit(solution)/shard_map/ppermute | solution.py:18
  368.4 10.2 %collective-permute-start.3 = (f32[1,1,4,16384]{3,2,0,1:T(4,128)S(1)}, f32[1,1,4,16384]{3,2,0,1:T(4,128)}, u32[]{:S(2)}, u32[]{:S(2)}) collective-permute-start(f32[1,1,4,16384]{3,2,0,1:T(4,128)S(1)} %get-tuple-element.11), channel_id=1, source_target_pairs={{1,0},{2,1},{3,2},{4,3},{5,4},{6,5},{7,6},{8,7},{9,8},{10,9},{11,1... | collective-permute-start | bytes 786440 | tf_op jit(solution)/shard_map/ppermute | solution.py:20
  378.6 3.6 copy-start.1
  382.0 1.3 copy-start.4
  382.0 58.0 %copy-start.13 = (f32[128]{0:T(128)S(1)}, f32[128]{0:T(128)}, u32[]{:S(2)}) copy-start(f32[128]{0:T(128)} %param.17) | copy-start | bytes 1540
  382.2 1.1 copy-start.2
  446.2 2.8 copy-start.7
  462.7 22.0 %copy-start.3 = (f32[1,16,16384]{2,1,0:T(8,128)S(1)}, f32[1,16,16384]{2,1,0:T(8,128)}, u32[]{:S(2)}) copy-start(f32[1,16,16384]{2,1,0:T(8,128)} %squeeze.32) | copy-start | bytes 3145732
  462.7 22.0 %copy-start.5 = (f32[1,16,16384]{2,1,0:T(8,128)S(1)}, f32[1,16,16384]{2,1,0:T(8,128)}, u32[]{:S(2)}) copy-start(f32[1,16,16384]{2,1,0:T(8,128)} %copy-done.4) | copy-start | bytes 3145732
  462.7 22.0 %copy-start.6 = (f32[1,16,16384]{2,1,0:T(8,128)S(1)}, f32[1,16,16384]{2,1,0:T(8,128)}, u32[]{:S(2)}) copy-start(f32[1,16,16384]{2,1,0:T(8,128)} %reshape.187) | copy-start | bytes 3145732
  465.2 9.9 %collective-permute-start.4 = (f32[1,1,4,16384]{3,2,0,1:T(4,128)S(1)}, f32[1,1,4,16384]{3,2,0,1:T(4,128)S(1)}, u32[]{:S(2)}, u32[]{:S(2)}) collective-permute-start(f32[1,1,4,16384]{3,2,0,1:T(4,128)S(1)} %get-tuple-element.6), channel_id=1, source_target_pairs={{0,32},{32,64},{64,96},{96,128},{128,160},{160,192},{192,224},{1,3... | collective-permute-start | bytes 786440 | tf_op jit(solution)/shard_map/ppermute | solution.py:18
  470.4 7.7 %collective-permute-start.5 = (f32[1,1,4,16384]{3,2,0,1:T(4,128)S(1)}, f32[1,1,4,16384]{3,2,0,1:T(4,128)S(1)}, u32[]{:S(2)}, u32[]{:S(2)}) collective-permute-start(f32[1,1,4,16384]{3,2,0,1:T(4,128)S(1)} %get-tuple-element.9), channel_id=1, source_target_pairs={{32,0},{64,32},{96,64},{128,96},{160,128},{192,160},{224,192},{33,... | collective-permute-start | bytes 786440 | tf_op jit(solution)/shard_map/ppermute | solution.py:20
  472.5 7.0 %collective-permute-start.6 = (f32[1,1,4,16384]{3,2,0,1:T(4,128)S(1)}, f32[1,1,4,16384]{3,2,0,1:T(4,128)S(1)}, u32[]{:S(2)}, u32[]{:S(2)}) collective-permute-start(f32[1,1,4,16384]{3,2,0,1:T(4,128)S(1)} %get-tuple-element.8), channel_id=1, source_target_pairs={{0,1},{1,2},{2,3},{3,4},{4,5},{5,6},{6,7},{7,8},{8,9},{9,10},{10,1... | collective-permute-start | bytes 786440 | tf_op jit(solution)/shard_map/ppermute | solution.py:18
  473.8 10.8 %collective-permute-start.7 = (f32[1,1,4,16384]{3,2,0,1:T(4,128)S(1)}, f32[1,1,4,16384]{3,2,0,1:T(4,128)S(1)}, u32[]{:S(2)}, u32[]{:S(2)}) collective-permute-start(f32[1,1,4,16384]{3,2,0,1:T(4,128)S(1)} %get-tuple-element.7), channel_id=1, source_target_pairs={{1,0},{2,1},{3,2},{4,3},{5,4},{6,5},{7,6},{8,7},{9,8},{10,9},{11,1... | collective-permute-start | bytes 786440 | tf_op jit(solution)/shard_map/ppermute | solution.py:20
Sparse Core Ops, SparseCore 0:
  12.7 211.5 reduce-scatter.1
